TPU v7x, 512 devices: a whole 4x8x8 slice. The times are simulated.
512 devices in a mesh: lat: 16 (over z, x_hi), lon: 32 (over y, x_lo, core).
Axes of the slice: x: 4 (x_hi: 2, x_lo: 2; x = x_hi * 2 + x_lo), y: 8, z: 8, core: 2. Of those that a mesh axis runs over, the one named last changes fastest.
Arguments:
- frame: bfloat16 [256, 512, 256], P('lat', 'lon'), may hold values from -64 to 64
- weight_qkv: bfloat16 [256, 768], replicated, may hold values from -0.375 to 0.375
- weight_proj: bfloat16 [256, 256], replicated, may hold values from -0.375 to 0.375
- gain_attn: float32 [256], replicated, may hold values from 0.5 to 1.5
- weight_up: bfloat16 [256, 1024], replicated, may hold values from -0.375 to 0.375
- weight_down: bfloat16 [1024, 256], replicated, may hold values from -0.1875 to 0.1875
- gain_mlp: float32 [256], replicated, may hold values from 0.5 to 1.5
- cotangent: bfloat16 [256, 512, 256], P('lat', 'lon'), may hold values from -6 to 6
Outputs:
- block_out: bfloat16 [256, 512, 256], P('lat', 'lon')
- grad_frame: bfloat16 [256, 512, 256], P('lat', 'lon')
- grad_qkv: bfloat16 [256, 768], replicated
- grad_proj: bfloat16 [256, 256], replicated
- grad_up: bfloat16 [256, 1024], replicated
- grad_down: bfloat16 [1024, 256], replicated
- grad_gain_attn: float32 [256], replicated
- grad_gain_mlp: float32 [256], replicated
All inputs are finite; a program needn't handle non-finite values.
Results may differ from a plain program's by a relative error of at most 0.012.
The roundings to bfloat16 on the way count: a program that leaves them out, or rounds other values in their place, can miss the bound.
Values may be sent and summed in bfloat16 or wider, within the bound.
No kernel may reach another device: no remote copies, remote signals or barrier semaphores. Data moves between devices by JAX's collectives and lax.ppermute only.
A program may use at most 128 MiB of HBM per device.

v0:
```python
import jax
import jax.numpy as jnp
from jax import lax
from jax.sharding import PartitionSpec as P

HEADS = 8
RADIUS = 6
epsilon = 1e-06
cubic_term = 0.044715
gelu_root = 0.7978845608028654
negative_big = -1e30


def padded_2(x, sides, width, wrap):
    for axis, dim in sides:
        devices, length = (lax.axis_size(axis), x.shape[dim])
        up = [(i, (i + 1) % devices) for i in range(devices if wrap else devices - 1)]
        down = [(j, i) for i, j in up]
        last = lax.slice_in_dim(x, length - width, length, axis=dim)
        first = lax.slice_in_dim(x, 0, width, axis=dim)
        before = lax.ppermute(last, axis, up)
        after = lax.ppermute(first, axis, down)
        x = jnp.concatenate([before, x, after], axis=dim)
    return x


def gelu_pair(upward):
    tangent = jnp.tanh(gelu_root * (upward + cubic_term * upward * upward * upward))
    activated = 0.5 * upward * (1.0 + tangent)
    derivative = 0.5 * (1.0 + tangent) + 0.5 * upward * (1.0 - tangent * tangent) * gelu_root * (
        1.0 + 3.0 * cubic_term * upward * upward
    )
    return (activated, derivative)


def rms_factor(field):
    return lax.rsqrt(jnp.mean(field * field, axis=-1, keepdims=True) + epsilon)


def norm_backward(incoming, field, factor):
    mean_term = jnp.mean(incoming * field, axis=-1, keepdims=True)
    return factor * (incoming - field * factor * factor * mean_term)


def contract_rows(left, right):
    return lax.dot_general(
        left, right, (((0,), (0,)), ((), ())), preferred_element_type=jnp.float32
    )


def contract_cols(left, right):
    return lax.dot_general(
        left, right, (((1,), (1,)), ((), ())), preferred_element_type=jnp.float32
    )


def row_strips(padded, rows, span):
    return jnp.stack(
        [lax.slice_in_dim(padded, offset, offset + rows, axis=0) for offset in range(span)], axis=1
    )


def unstrip(strip_sum, rows, span):
    total = jnp.zeros((rows + span - 1,) + strip_sum.shape[2:], strip_sum.dtype)
    for offset in range(span):
        total = total.at[offset : offset + rows].add(strip_sum[:, offset])
    return total


def fold_rims(field, axis, length, radius):
    middle = lax.slice_in_dim(field, 2 * radius, 2 * radius + length, axis=axis)
    front = lax.slice_in_dim(field, 0, radius, axis=axis)
    back = lax.slice_in_dim(field, length + 3 * radius, length + 4 * radius, axis=axis)
    widths_front = [(0, 0)] * field.ndim
    widths_front[axis] = (0, length - radius)
    widths_back = [(0, 0)] * field.ndim
    widths_back[axis] = (length - radius, 0)
    return middle + jnp.pad(front, widths_front) + jnp.pad(back, widths_back)


def band_strips(padded, rows, span, heads):
    strips = row_strips(padded, rows, span)
    return strips.reshape(rows, span * padded.shape[1], heads, padded.shape[2] // heads)


def on_device(
    frame, weight_qkv, weight_proj, gain_attn, weight_up, weight_down, gain_mlp, cotangent
):
    lat_rows, lon_cols, width = frame.shape
    heads = HEADS
    head_size = width // heads
    radius = RADIUS
    span = 2 * radius + 1
    head_scale = head_size ** (-0.5)
    pad_rows = lat_rows + 2 * radius
    pad_cols = lon_cols + 2 * radius
    band = span * pad_cols
    local_tokens = lat_rows * lon_cols
    lat_total = lat_rows * lax.axis_size("lat")
    tokens_all = lat_total * lon_cols * lax.axis_size("lon")
    grad_scale = tokens_all ** (-0.5)
    lat_first = lax.axis_index("lat") * lat_rows
    row_global = lat_first + jnp.arange(lat_rows)[:, None] + jnp.arange(span)[None, :] - radius
    row_ok = (row_global >= 0) & (row_global < lat_total)
    col_gap = jnp.arange(pad_cols)[None, :] - radius - jnp.arange(lon_cols)[:, None]
    near = jnp.abs(col_gap) <= radius
    valid = (row_ok[:, None, :, None] & near[None, :, None, :]).reshape(lat_rows, 1, lon_cols, band)
    flat = frame.reshape(local_tokens, width)
    projected = jnp.dot(flat, weight_qkv, preferred_element_type=jnp.float32).astype(jnp.bfloat16)
    queries = projected[:, :width]
    pairs = projected[:, width:].reshape(lat_rows, lon_cols, 2 * width)
    widened = padded_2(pairs, (("lon", 1),), radius, True)
    margined = padded_2(widened, (("lat", 0),), radius, False)
    pair_pad = margined.reshape(-1, 2 * width)
    queries4 = queries.reshape(lat_rows, lon_cols, heads, head_size)
    keys_pad = pair_pad[:, :width].reshape(pad_rows, pad_cols, width)
    values_pad = pair_pad[:, width:].reshape(pad_rows, pad_cols, width)
    key_strip = band_strips(keys_pad, lat_rows, span, heads)
    value_strip = band_strips(values_pad, lat_rows, span, heads)
    scores = (
        jnp.einsum("ichd,inhd->ihcn", queries4, key_strip, preferred_element_type=jnp.float32)
        * head_scale
    )
    scores = jnp.where(valid, scores, negative_big)
    peak = jnp.max(scores, axis=3, keepdims=True)
    expo = jnp.exp(scores - peak)
    total = jnp.sum(expo, axis=3, keepdims=True)
    probs = expo / total
    probs_bf = probs.astype(jnp.bfloat16)
    attended = (
        jnp.einsum("ihcn,inhd->ichd", probs_bf, value_strip, preferred_element_type=jnp.float32)
        .astype(jnp.bfloat16)
        .reshape(local_tokens, width)
    )
    proj = jnp.dot(attended, weight_proj, preferred_element_type=jnp.float32)
    factor_one = rms_factor(proj)
    mid = (flat.astype(jnp.float32) + proj * factor_one * gain_attn).astype(jnp.bfloat16)
    upward = jnp.dot(mid, weight_up, preferred_element_type=jnp.float32)
    activated, derivative = gelu_pair(upward)
    hidden = activated.astype(jnp.bfloat16)
    downward = jnp.dot(hidden, weight_down, preferred_element_type=jnp.float32)
    factor_two = rms_factor(downward)
    block_out = (mid.astype(jnp.float32) + downward * factor_two * gain_mlp).astype(jnp.bfloat16)
    incoming = cotangent.reshape(local_tokens, width).astype(jnp.float32)
    local_gain_mlp = jnp.sum(incoming * downward * factor_two, axis=0)
    d_down = norm_backward(incoming * gain_mlp, downward, factor_two).astype(jnp.bfloat16)
    local_down = contract_rows(hidden, d_down)
    d_up = (contract_cols(d_down, weight_down) * derivative).astype(jnp.bfloat16)
    local_up = contract_rows(mid, d_up)
    d_mid = incoming + contract_cols(d_up, weight_up)
    local_gain_attn = jnp.sum(d_mid * proj * factor_one, axis=0)
    d_proj = norm_backward(d_mid * gain_attn, proj, factor_one).astype(jnp.bfloat16)
    local_proj = contract_rows(attended, d_proj)
    d_attended = contract_cols(d_proj, weight_proj).astype(jnp.bfloat16)
    d_attended4 = d_attended.reshape(lat_rows, lon_cols, heads, head_size)
    d_probs = jnp.einsum(
        "ichd,inhd->ihcn", d_attended4, value_strip, preferred_element_type=jnp.float32
    )
    d_weighted = jnp.sum(probs * d_probs, axis=3, keepdims=True)
    d_scores = (probs * (d_probs - d_weighted) * head_scale).astype(jnp.bfloat16)
    d_queries = jnp.einsum(
        "ihcn,inhd->ichd", d_scores, key_strip, preferred_element_type=jnp.float32
    ).reshape(local_tokens, width)
    key_terms = jnp.einsum(
        "ihcn,ichd->inhd", d_scores, queries4, preferred_element_type=jnp.float32
    ).reshape(lat_rows, span, pad_cols, width)
    value_terms = jnp.einsum(
        "ihcn,ichd->inhd", probs_bf, d_attended4, preferred_element_type=jnp.float32
    ).reshape(lat_rows, span, pad_cols, width)
    pair_grads = unstrip(jnp.concatenate([key_terms, value_terms], axis=3), lat_rows, span)
    widened_grads = padded_2(pair_grads.astype(jnp.bfloat16), (("lon", 1),), radius, True).astype(
        pair_grads.dtype
    )
    margined_grads = padded_2(
        widened_grads.astype(jnp.bfloat16), (("lat", 0),), radius, False
    ).astype(widened_grads.dtype)
    owned = fold_rims(fold_rims(margined_grads, 0, lat_rows, radius), 1, lon_cols, radius).reshape(
        local_tokens, 2 * width
    )
    d_projected = jnp.concatenate([d_queries, owned], axis=1).astype(jnp.bfloat16)
    local_qkv = contract_rows(flat, d_projected)
    grad_frame = (d_mid + contract_cols(d_projected, weight_qkv)).astype(jnp.bfloat16)
    sum_qkv, sum_proj, sum_up, sum_down, sum_gain_attn, sum_gain_mlp = lax.psum(
        (local_qkv, local_proj, local_up, local_down, local_gain_attn, local_gain_mlp),
        ("lat", "lon"),
    )
    return (
        block_out.reshape(lat_rows, lon_cols, width),
        grad_frame.reshape(lat_rows, lon_cols, width),
        (sum_qkv * grad_scale).astype(jnp.bfloat16),
        (sum_proj * grad_scale).astype(jnp.bfloat16),
        (sum_up * grad_scale).astype(jnp.bfloat16),
        (sum_down * grad_scale).astype(jnp.bfloat16),
        sum_gain_attn * grad_scale,
        sum_gain_mlp * grad_scale,
    )


def solution(mesh):
    return jax.shard_map(
        on_device,
        mesh=mesh,
        in_specs=(P("lat", "lon", None), P(), P(), P(), P(), P(), P(), P("lat", "lon", None)),
        out_specs=(P("lat", "lon", None), P("lat", "lon", None), P(), P(), P(), P(), P(), P()),
        check_vma=False,
    )
```

profile of v0, /device:TPU:17, one launch (start us, length us, event | category | flops | bytes accessed | tf_op | source)
XLA Modules:
  0.0 695.6 jit_solution(14059497985502001922)
XLA Ops:
  8.7 3.7 collective-permute-start
  15.1 3.6 collective-permute-done.1
  18.8 4.4 collective-permute-start.2
  27.4 5.3 collective-permute-done.3
  79.8 18.8 %copy.50 = bf16[16,13,28,256]{2,1,3,0:T(8,128)(2,1)} copy(bf16[16,13,28,256]{3,2,0,1:T(8,128)(2,1)} %constant_dynamic-update-slice_fusion.13) | data formatting | bytes 5963776 | tf_op jit(solution)/shard_map/reshape | solution.py:83
  98.6 21.2 %reshape.626 = bf16[16,364,8,32]{1,3,2,0:T(8,128)(2,1)} reshape(bf16[16,13,28,256]{2,1,3,0:T(8,128)(2,1)} %copy.50) | data formatting | bytes 5963776 | tf_op jit(solution)/shard_map/reshape | solution.py:83
  128.6 18.8 %copy.49 = bf16[16,13,28,256]{2,1,3,0:T(8,128)(2,1)} copy(bf16[16,13,28,256]{3,2,0,1:T(8,128)(2,1)} %constant_dynamic-update-slice_fusion) | data formatting | bytes 5963776 | tf_op jit(solution)/shard_map/reshape | solution.py:83
  147.4 21.2 %reshape.625 = bf16[16,364,8,32]{1,3,2,0:T(8,128)(2,1)} reshape(bf16[16,13,28,256]{2,1,3,0:T(8,128)(2,1)} %copy.49) | data formatting | bytes 5963776 | tf_op jit(solution)/shard_map/reshape | solution.py:83
  171.2 3.8 fusion.78
  182.0 4.3 fusion.49
  186.3 17.5 %fusion.20 = bf16[16,16,8,32]{3,1,2,0:T(8,128)(2,1)} fusion(bf16[16,364,8,32]{1,3,2,0:T(8,128)(2,1)} %reshape.626, f32[16,8,16,364]{3,2,1,0:T(8,128)} %fusion.49, f32[16,8,16,364]{3,2,1,0:T(8,128)} %copy-done.5, f32[16,8,16]{2,1,0:T(8,128)S(1)} %get-tuple-element.226), kind=kOutput, calls=%fused_computation.27 | convolution fusion | flops 52996460 | bytes 9084928 | tf_op jit(solution)/shard_map/ihcn,inhd->ichd/dot_general | solution.py:161
  203.8 17.6 %convolution_bitcast_fusion.1 = f32[16,364,8,32]{1,3,2,0:T(8,128)} fusion(f32[16,8,16,364]{3,2,1,0:T(8,128)} %fusion.49, bf16[16,16,8,32]{3,2,1,0:T(8,128)(2,1)S(1)} %reshape.602, f32[16,8,16,364]{3,2,1,0:T(8,128)} %copy-done.5, f32[16,8,16]{2,1,0:T(8,128)S(1)} %get-tuple-element.226), kind=kOutput, calls=%fused_computation.8 | convolution fusion | flops 52930924 | bytes 12066816 | tf_op jit(solution)/shard_map/ihcn,ichd->inhd/dot_general | solution.py:164
  221.3 5.6 convolution_bitcast_fusion
  226.9 20.3 %copy.46 = f32[16,364,8,32]{3,2,0,1:T(8,128)} copy(f32[16,364,8,32]{1,3,2,0:T(8,128)} %convolution_bitcast_fusion) | data formatting | bytes 11927552 | tf_op jit(solution)/shard_map/ihcn,ichd->inhd/transpose | solution.py:167
  247.3 16.9 %reshape.609 = f32[16,13,28,256]{3,0,2,1:T(8,128)} reshape(f32[16,364,8,32]{3,2,0,1:T(8,128)} %copy.46) | data formatting | bytes 11927552 | tf_op jit(solution)/shard_map/reshape | solution.py:169
  264.2 20.3 %copy.44 = f32[16,364,8,32]{3,2,0,1:T(8,128)} copy(f32[16,364,8,32]{1,3,2,0:T(8,128)} %convolution_bitcast_fusion.1) | data formatting | bytes 11927552 | tf_op jit(solution)/shard_map/ihcn,ichd->inhd/transpose | solution.py:164
  284.5 16.8 %reshape.608 = f32[16,13,28,256]{3,0,2,1:T(8,128)} reshape(f32[16,364,8,32]{3,2,0,1:T(8,128)} %copy.44) | data formatting | bytes 11927552 | tf_op jit(solution)/shard_map/reshape | solution.py:166
  301.3 3.8 constant_dynamic-update-slice_fusion.27
  307.7 4.1 copy-done.2
  360.1 3.7 collective-permute-done.5
  364.8 5.1 collective-permute-start.6
  374.2 9.6 %collective-permute-done.6 = bf16[6,40,512]{2,0,1:T(8,128)(2,1)S(1)} collective-permute-done((bf16[6,40,512]{2,0,1:T(8,128)(2,1)}, bf16[6,40,512]{2,0,1:T(8,128)(2,1)S(1)}, u32[]{:S(2)}, u32[]{:S(2)}) %collective-permute-start.6) | collective-permute-done | bytes 245792 | tf_op jit(solution)/shard_map/ppermute | solution.py:21
  386.7 106.6 %all-reduce.3 = (f32[256]{0:T(256)S(1)}, f32[256]{0:T(256)S(1)}) all-reduce(f32[256]{0:T(256)S(1)} %get-tuple-element.180, f32[256]{0:T(256)S(1)} %get-tuple-element.182), channel_id=1, replica_groups=mesh['lat'=16,'lon'=32] {'lat','lon'}, use_global_device_ids=true, to_apply=%region_12.13 | all-reduce | flops 512 | bytes 4096 | tf_op jit(solution)/shard_map/psum | solution.py:183
  494.9 186.8 %all-reduce.7.cloned.1.call-done = (f32[256,768]{0,1:T(8,128)}, f32[256,256]{1,0:T(8,128)}, f32[256,1024]{1,0:T(8,128)}, f32[1024,256]{1,0:T(8,128)}) async-done(((f32[256,768]{0,1:T(8,128)}, f32[256,256]{1,0:T(8,128)}, f32[256,1024]{1,0:T(8,128)}, f32[1024,256]{1,0:T(8,128)}), (f32[256,768]{0,1:T(8,128)}, f32[256,256]{1,0:T(8,128)}, f32[256,1024]{1,0:T(8,128)}, ...) | async-done | bytes 3145744 | tf_op jit(solution)/shard_map/psum | solution.py:183
  (234 shorter events, 140.5 us)
Async XLA Ops:
  7.2 170.5 %copy-start = (bf16[256,1024]{1,0:T(8,128)(2,1)S(1)}, bf16[256,1024]{1,0:T(8,128)(2,1)}, u32[]{:S(2)}) copy-start(bf16[256,1024]{1,0:T(8,128)(2,1)} %param.38) | copy-start | bytes 1572868
  7.2 674.5 %all-reduce.7.cloned.1.call-start = ((), (), s32[]{:S(2)}) async-start(), calls=%async_computation | async-start | bytes 6291456 | tf_op jit(solution)/shard_map/psum | solution.py:183
  8.7 6.4 collective-permute-start
  12.4 6.3 collective-permute-start.1
  18.8 8.6 %collective-permute-start.2 = (bf16[6,28,512]{2,1,0:T(8,128)(2,1)S(1)}, bf16[6,28,512]{2,1,0:T(8,128)(2,1)S(1)}, u32[]{:S(2)}, u32[]{:S(2)}) collective-permute-start(bf16[6,28,512]{2,1,0:T(8,128)(2,1)S(1)} %get-tuple-element.220), channel_id=1, source_target_pairs={{0,32},{32,64},{64,96},{96,128},{128,160},{160,192},{192,224},{224... | collective-permute-start | bytes 516104 | tf_op jit(solution)/shard_map/ppermute | solution.py:21
  23.2 9.6 %collective-permute-start.3 = (bf16[6,28,512]{2,1,0:T(8,128)(2,1)S(1)}, bf16[6,28,512]{2,1,0:T(8,128)(2,1)S(1)}, u32[]{:S(2)}, u32[]{:S(2)}) collective-permute-start(bf16[6,28,512]{2,1,0:T(8,128)(2,1)S(1)} %get-tuple-element.221), channel_id=1, source_target_pairs={{32,0},{64,32},{96,64},{128,96},{160,128},{192,160},{224,192},{256... | collective-permute-start | bytes 516104 | tf_op jit(solution)/shard_map/ppermute | solution.py:22
  38.1 19.4 %copy-start.31 = (bf16[448,256]{1,0:T(8,128)(2,1)S(1)}, bf16[448,256]{1,0:T(8,128)(2,1)}, u32[]{:S(2)}) copy-start(bf16[448,256]{1,0:T(8,128)(2,1)} %get-tuple-element.206) | copy-start | bytes 688132
  38.1 20.1 %copy-start.30 = (bf16[448,256]{1,0:T(8,128)(2,1)S(1)}, bf16[448,256]{1,0:T(8,128)(2,1)}, u32[]{:S(2)}) copy-start(bf16[448,256]{1,0:T(8,128)(2,1)} %get-tuple-element.207) | copy-start | bytes 688132
  38.9 19.4 %copy-start.29 = (bf16[448,256]{1,0:T(8,128)(2,1)S(1)}, bf16[448,256]{1,0:T(8,128)(2,1)}, u32[]{:S(2)}) copy-start(bf16[448,256]{1,0:T(8,128)(2,1)} %get-tuple-element.208) | copy-start | bytes 688132
  64.5 12.4 %copy-start.23 = (bf16[16,1,28,256]{3,2,0,1:T(8,128)(2,1)S(1)}, bf16[16,1,28,256]{3,2,0,1:T(8,128)(2,1)}, u32[]{:S(2)}) copy-start(bf16[16,1,28,256]{3,2,0,1:T(8,128)(2,1)} %stack.107) | copy-start | bytes 688132
  64.5 13.1 %copy-start.21 = (bf16[16,1,28,256]{3,2,0,1:T(8,128)(2,1)S(1)}, bf16[16,1,28,256]{3,2,0,1:T(8,128)(2,1)}, u32[]{:S(2)}) copy-start(bf16[16,1,28,256]{3,2,0,1:T(8,128)(2,1)} %stack.108) | copy-start | bytes 688132
  64.5 13.9 %copy-start.19 = (bf16[16,1,28,256]{3,2,0,1:T(8,128)(2,1)S(1)}, bf16[16,1,28,256]{3,2,0,1:T(8,128)(2,1)}, u32[]{:S(2)}) copy-start(bf16[16,1,28,256]{3,2,0,1:T(8,128)(2,1)} %stack.109) | copy-start | bytes 688132
  64.5 14.6 %copy-start.17 = (bf16[16,1,28,256]{3,2,0,1:T(8,128)(2,1)S(1)}, bf16[16,1,28,256]{3,2,0,1:T(8,128)(2,1)}, u32[]{:S(2)}) copy-start(bf16[16,1,28,256]{3,2,0,1:T(8,128)(2,1)} %stack.110) | copy-start | bytes 688132
  353.2 18.2 %copy-start.7 = (bf16[256,1024]{1,0:T(8,128)(2,1)S(1)}, bf16[256,1024]{1,0:T(8,128)(2,1)}, u32[]{:S(2)}) copy-start(bf16[256,1024]{1,0:T(8,128)(2,1)} %copy-done.6) | copy-start | bytes 1572868
  353.3 6.8 collective-permute-start.4
  355.3 17.4 %copy-start.33 = (bf16[16,16,8,32]{3,1,2,0:T(8,128)(2,1)S(1)}, bf16[16,16,8,32]{3,1,2,0:T(8,128)(2,1)}, u32[]{:S(2)}) copy-start(bf16[16,16,8,32]{3,1,2,0:T(8,128)(2,1)} %fusion.20) | copy-start | bytes 393220
  355.3 8.5 %collective-permute-start.5 = (bf16[28,6,512]{2,0,1:T(8,128)(2,1)S(1)}, bf16[28,6,512]{2,0,1:T(8,128)(2,1)S(1)}, u32[]{:S(2)}, u32[]{:S(2)}) collective-permute-start(bf16[28,6,512]{2,0,1:T(8,128)(2,1)S(1)} %get-tuple-element.193), channel_id=1, source_target_pairs={{1,0},{2,1},{3,2},{4,3},{5,4},{6,5},{7,6},{8,7},{9,8},{10,9},{11,1... | collective-permute-start | bytes 516104 | tf_op jit(solution)/shard_map/ppermute | solution.py:22
  360.1 13.1 %copy-start.10 = (bf16[256,256]{1,0:T(8,128)(2,1)S(1)}, bf16[256,256]{1,0:T(8,128)(2,1)}, u32[]{:S(2)}) copy-start(bf16[256,256]{1,0:T(8,128)(2,1)} %copy-done.9) | copy-start | bytes 393220
  360.1 13.1 %copy-start.12 = (bf16[256,256]{1,0:T(8,128)(2,1)S(1)}, bf16[256,256]{1,0:T(8,128)(2,1)}, u32[]{:S(2)}) copy-start(bf16[256,256]{1,0:T(8,128)(2,1)} %copy-done.11) | copy-start | bytes 393220
  364.8 19.0 %collective-permute-start.6 = (bf16[6,40,512]{2,0,1:T(8,128)(2,1)}, bf16[6,40,512]{2,0,1:T(8,128)(2,1)S(1)}, u32[]{:S(2)}, u32[]{:S(2)}) collective-permute-start(bf16[6,40,512]{2,0,1:T(8,128)(2,1)} %get-tuple-element.190), channel_id=1, source_target_pairs={{0,32},{32,64},{64,96},{96,128},{128,160},{160,192},{192,224},{224... | collective-permute-start | bytes 737288 | tf_op jit(solution)/shard_map/ppermute | solution.py:21
  369.9 13.9 %collective-permute-start.7 = (bf16[6,40,512]{2,0,1:T(8,128)(2,1)}, bf16[6,40,512]{2,0,1:T(8,128)(2,1)S(1)}, u32[]{:S(2)}, u32[]{:S(2)}) collective-permute-start(bf16[6,40,512]{2,0,1:T(8,128)(2,1)} %get-tuple-element.191), channel_id=1, source_target_pairs={{32,0},{64,32},{96,64},{128,96},{160,128},{192,160},{224,192},{256... | collective-permute-start | bytes 737288 | tf_op jit(solution)/shard_map/ppermute | solution.py:22
  385.1 108.8 %copy-start.16 = (f32[256,256]{1,0:T(8,128)S(1)}, f32[256,256]{1,0:T(8,128)}, u32[]{:S(2)}) copy-start(f32[256,256]{1,0:T(8,128)} %copy-done.15) | copy-start | bytes 786436
  385.1 108.8 %copy-start.35 = (bf16[256,768]{1,0:T(8,128)(2,1)S(1)}, bf16[256,768]{1,0:T(8,128)(2,1)}, u32[]{:S(2)}) copy-start(bf16[256,768]{1,0:T(8,128)(2,1)} %param.35) | copy-start | bytes 1179652
  493.3 195.2 %copy-start.1 = (bf16[256,1024]{1,0:T(8,128)(2,1)S(1)}, bf16[256,1024]{1,0:T(8,128)(2,1)}, u32[]{:S(2)}) copy-start(bf16[256,1024]{1,0:T(8,128)(2,1)} %param.38) | copy-start | bytes 1572868
  (28 other events, 106.1 us)
Sparse Core Ops, SparseCore 0:
  386.8 294.7 all-reduce.6
where the time goes:
time: 707 us; the launch traced here: 696 us
  local copies, waits for them, and re-layouts  249 us (35%)
  waiting for transfers between devices  211 us (30%)
  blocking collectives  107 us (15%)
  matrix products  58.8 us (8%)
  other arithmetic  31.2 us (4%)
  starting transfers between devices  23.1 us (3%)
  between operations  15.2 us (2%)
    psum x1, waiting for transfers between devices, on_device(): lax.psum((local_qkv, local_proj, local_up, local_down, local_gain_attn, l...  187 us
    psum x1, blocking collectives, on_device(): lax.psum((local_qkv, local_proj, local_up, local_down, local_gain_attn, l...  107 us
    reshape x4, local copies, waits for them, and re-layouts, band_strips(): strips.reshape(rows, span * padded.shape[1], heads, padded.shape[2] // he...  80.1 us
    unnamed x112, local copies, waits for them, and re-layouts  33.7 us
    another operation x28, local copies, waits for them, and re-layouts, row_strips(): jnp.stack([lax.slice_in_dim(padded, offset, offset + rows, axis=0) for of...  29 us
    scatter-add x12, local copies, waits for them, and re-layouts, unstrip(): total = total.at[offset:offset + rows].add(strip_sum[:, offset])  25.4 us
    transpose x1, local copies, waits for them, and re-layouts, on_device(): jnp.einsum('ihcn,ichd->inhd', probs_bf, d_attended4, preferred_element_ty...  20.3 us
    transpose x1, local copies, waits for them, and re-layouts, on_device(): jnp.einsum('ihcn,ichd->inhd', d_scores, queries4, preferred_element_type=...  20.3 us
  transfers between devices with their start and end apart: 9, of which 6 were waited for; matrix products, arithmetic and copies ran while one was open for 1% of the time, Pallas kernels for 0%

commit v1 on v0

--- a/solution.py
+++ b/solution.py
@@ -9,6 +9,12 @@
 cubic_term = 0.044715
 gelu_root = 0.7978845608028654
 negative_big = -1e30
+
+
+def chains_push(local_x, axis_key, chip_axis):
+    for idx in (axis_key, chip_axis):
+        local_x = lax.psum(local_x, idx)
+    return local_x
 
 
 def padded_2(x, sides, width, wrap):
@@ -180,9 +186,8 @@
     d_projected = jnp.concatenate([d_queries, owned], axis=1).astype(jnp.bfloat16)
     local_qkv = contract_rows(flat, d_projected)
     grad_frame = (d_mid + contract_cols(d_projected, weight_qkv)).astype(jnp.bfloat16)
-    sum_qkv, sum_proj, sum_up, sum_down, sum_gain_attn, sum_gain_mlp = lax.psum(
-        (local_qkv, local_proj, local_up, local_down, local_gain_attn, local_gain_mlp),
-        ("lat", "lon"),
+    sum_qkv, sum_proj, sum_up, sum_down, sum_gain_attn, sum_gain_mlp = chains_push(
+        (local_qkv, local_proj, local_up, local_down, local_gain_attn, local_gain_mlp), "lat", "lon"
     )
     return (
         block_out.reshape(lat_rows, lon_cols, width),

time: 707 us -> 851 us (1.20)
  the two profiles are of different devices: /device:TPU:17 before, /device:TPU:1 now
where the time goes in v1:
time: 851 us; the launch traced here: 839 us
  waiting for transfers between devices  351 us (41%)
  local copies, waits for them, and re-layouts  249 us (29%)
  blocking collectives  100 us (12%)
  matrix products  58.8 us (7%)
  starting transfers between devices  34 us (4%)
  other arithmetic  31.2 us (4%)
  between operations  15.2 us (2%)
    psum x2, waiting for transfers between devices, chains_push(): local_x = lax.psum(local_x, idx)  334 us
    psum x2, blocking collectives, chains_push(): local_x = lax.psum(local_x, idx)  100 us
    reshape x4, local copies, waits for them, and re-layouts, band_strips(): strips.reshape(rows, span * padded.shape[1], heads, padded.shape[2] // he...  80.1 us
    unnamed x112, local copies, waits for them, and re-layouts  33.7 us
    another operation x28, local copies, waits for them, and re-layouts, row_strips(): jnp.stack([lax.slice_in_dim(padded, offset, offset + rows, axis=0) for of...  29 us
    scatter-add x12, local copies, waits for them, and re-layouts, unstrip(): total = total.at[offset:offset + rows].add(strip_sum[:, offset])  25.4 us
    transpose x1, local copies, waits for them, and re-layouts, on_device(): jnp.einsum('ihcn,ichd->inhd', probs_bf, d_attended4, preferred_element_ty...  20.3 us
    transpose x1, local copies, waits for them, and re-layouts, on_device(): jnp.einsum('ihcn,ichd->inhd', d_scores, queries4, preferred_element_type=...  20.3 us
  transfers between devices with their start and end apart: 10, of which 7 were waited for; matrix products, arithmetic and copies ran while one was open for 1% of the time, Pallas kernels for 0%

profile of v1, /device:TPU:1, one launch (start us, length us, event | category | flops | bytes accessed | tf_op | source)
XLA Modules:
  0.0 839.2 jit_solution(13527819728000456693)
XLA Ops:
  8.7 4.5 collective-permute-start
  13.2 6.2 collective-permute-start.1
  26.7 5.3 collective-permute-done.3
  79.0 18.8 %copy.50 = bf16[16,13,28,256]{2,1,3,0:T(8,128)(2,1)} copy(bf16[16,13,28,256]{3,2,0,1:T(8,128)(2,1)} %constant_dynamic-update-slice_fusion.13) | data formatting | bytes 5963776 | tf_op jit(solution)/shard_map/reshape | solution.py:89
  97.9 21.2 %reshape.626 = bf16[16,364,8,32]{1,3,2,0:T(8,128)(2,1)} reshape(bf16[16,13,28,256]{2,1,3,0:T(8,128)(2,1)} %copy.50) | data formatting | bytes 5963776 | tf_op jit(solution)/shard_map/reshape | solution.py:89
  127.8 18.8 %copy.49 = bf16[16,13,28,256]{2,1,3,0:T(8,128)(2,1)} copy(bf16[16,13,28,256]{3,2,0,1:T(8,128)(2,1)} %constant_dynamic-update-slice_fusion) | data formatting | bytes 5963776 | tf_op jit(solution)/shard_map/reshape | solution.py:89
  146.6 21.2 %reshape.625 = bf16[16,364,8,32]{1,3,2,0:T(8,128)(2,1)} reshape(bf16[16,13,28,256]{2,1,3,0:T(8,128)(2,1)} %copy.49) | data formatting | bytes 5963776 | tf_op jit(solution)/shard_map/reshape | solution.py:89
  170.5 3.8 fusion.78
  181.2 4.3 fusion.49
  185.5 17.5 %fusion.20 = bf16[16,16,8,32]{3,1,2,0:T(8,128)(2,1)} fusion(bf16[16,364,8,32]{1,3,2,0:T(8,128)(2,1)} %reshape.626, f32[16,8,16,364]{3,2,1,0:T(8,128)} %fusion.49, f32[16,8,16,364]{3,2,1,0:T(8,128)} %copy-done.5, f32[16,8,16]{2,1,0:T(8,128)S(1)} %get-tuple-element.232), kind=kOutput, calls=%fused_computation.27 | convolution fusion | flops 52996460 | bytes 9084928 | tf_op jit(solution)/shard_map/ihcn,inhd->ichd/dot_general | solution.py:167
  203.0 17.6 %convolution_bitcast_fusion.1 = f32[16,364,8,32]{1,3,2,0:T(8,128)} fusion(f32[16,8,16,364]{3,2,1,0:T(8,128)} %fusion.49, bf16[16,16,8,32]{3,2,1,0:T(8,128)(2,1)S(1)} %reshape.602, f32[16,8,16,364]{3,2,1,0:T(8,128)} %copy-done.5, f32[16,8,16]{2,1,0:T(8,128)S(1)} %get-tuple-element.232), kind=kOutput, calls=%fused_computation.8 | convolution fusion | flops 52930924 | bytes 12066816 | tf_op jit(solution)/shard_map/ihcn,ichd->inhd/dot_general | solution.py:170
  220.6 5.6 convolution_bitcast_fusion
  226.2 20.3 %copy.46 = f32[16,364,8,32]{3,2,0,1:T(8,128)} copy(f32[16,364,8,32]{1,3,2,0:T(8,128)} %convolution_bitcast_fusion) | data formatting | bytes 11927552 | tf_op jit(solution)/shard_map/ihcn,ichd->inhd/transpose | solution.py:173
  246.5 16.9 %reshape.609 = f32[16,13,28,256]{3,0,2,1:T(8,128)} reshape(f32[16,364,8,32]{3,2,0,1:T(8,128)} %copy.46) | data formatting | bytes 11927552 | tf_op jit(solution)/shard_map/reshape | solution.py:175
  263.4 20.3 %copy.44 = f32[16,364,8,32]{3,2,0,1:T(8,128)} copy(f32[16,364,8,32]{1,3,2,0:T(8,128)} %convolution_bitcast_fusion.1) | data formatting | bytes 11927552 | tf_op jit(solution)/shard_map/ihcn,ichd->inhd/transpose | solution.py:170
  283.8 16.8 %reshape.608 = f32[16,13,28,256]{3,0,2,1:T(8,128)} reshape(f32[16,364,8,32]{3,2,0,1:T(8,128)} %copy.44) | data formatting | bytes 11927552 | tf_op jit(solution)/shard_map/reshape | solution.py:172
  307.0 4.1 copy-done.2
  355.7 5.2 collective-permute-start.5
  363.7 8.5 %collective-permute-start.6 = (bf16[6,40,512]{2,0,1:T(8,128)(2,1)}, bf16[6,40,512]{2,0,1:T(8,128)(2,1)S(1)}, u32[]{:S(2)}, u32[]{:S(2)}) collective-permute-start(bf16[6,40,512]{2,0,1:T(8,128)(2,1)} %get-tuple-element.196), channel_id=1, source_target_pairs={{0,32},{32,64},{64,96},{96,128},{128,160},{160,192},{192,224},{224... | collective-permute-start | bytes 737288 | tf_op jit(solution)/shard_map/ppermute | solution.py:27
  376.5 9.6 %collective-permute-done.6 = bf16[6,40,512]{2,0,1:T(8,128)(2,1)S(1)} collective-permute-done((bf16[6,40,512]{2,0,1:T(8,128)(2,1)}, bf16[6,40,512]{2,0,1:T(8,128)(2,1)S(1)}, u32[]{:S(2)}, u32[]{:S(2)}) %collective-permute-start.6) | collective-permute-done | bytes 245792 | tf_op jit(solution)/shard_map/ppermute | solution.py:27
  389.1 187.2 %all-reduce.12.cloned.1.call-done = (f32[256,768]{0,1:T(8,128)}, f32[256,256]{1,0:T(8,128)}, f32[256,1024]{1,0:T(8,128)}, f32[1024,256]{1,0:T(8,128)}) async-done(((f32[256,768]{0,1:T(8,128)}, f32[256,256]{1,0:T(8,128)}, f32[256,1024]{1,0:T(8,128)}, f32[1024,256]{1,0:T(8,128)}), (f32[256,768]{0,1:T(8,128)}, f32[256,256]{1,0:T(8,128)}, f32[256,1024]{1,0:T(8,128)}, ...) | async-done | bytes 3145744 | tf_op jit(solution)/shard_map/psum | solution.py:16
  576.3 31.1 %all-reduce.5 = (f32[256]{0:T(256)S(1)}, f32[256]{0:T(256)S(1)}) all-reduce(f32[256]{0:T(256)S(1)} %get-tuple-element.180, f32[256]{0:T(256)S(1)} %get-tuple-element.182), channel_id=1, replica_groups=mesh['lat'=16,'lon'=32] {'lat'}, use_global_device_ids=true, to_apply=%region_16.17 | all-reduce | flops 512 | bytes 4096 | tf_op jit(solution)/shard_map/psum | solution.py:16
  607.4 69.0 %all-reduce.3 = (f32[256]{0:T(256)S(1)}, f32[256]{0:T(256)S(1)}) all-reduce(f32[256]{0:T(256)S(1)} %get-tuple-element.190, f32[256]{0:T(256)S(1)} %get-tuple-element.191), channel_id=1, replica_groups=mesh['lat'=16,'lon'=32] {'lon'}, use_global_device_ids=true, to_apply=%region_17.18 | all-reduce | flops 512 | bytes 4096 | tf_op jit(solution)/shard_map/psum | solution.py:16
  678.0 147.3 %all-reduce.10.cloned.1.call-done = (f32[256,768]{0,1:T(8,128)}, f32[256,256]{1,0:T(8,128)}, f32[256,1024]{1,0:T(8,128)}, f32[1024,256]{1,0:T(8,128)}) async-done(((f32[256,768]{0,1:T(8,128)}, f32[256,256]{1,0:T(8,128)}, f32[256,1024]{1,0:T(8,128)}, f32[1024,256]{1,0:T(8,128)}), (f32[256,768]{0,1:T(8,128)}, f32[256,256]{1,0:T(8,128)}, f32[256,1024]{1,0:T(8,128)}, ...) | async-done | bytes 3145744 | tf_op jit(solution)/shard_map/psum | solution.py:16
  (238 shorter events, 142.8 us)
Async XLA Ops:
  7.2 169.7 %copy-start = (bf16[256,1024]{1,0:T(8,128)(2,1)S(1)}, bf16[256,1024]{1,0:T(8,128)(2,1)}, u32[]{:S(2)}) copy-start(bf16[256,1024]{1,0:T(8,128)(2,1)} %param.38) | copy-start | bytes 1572868
  7.2 569.1 %all-reduce.12.cloned.1.call-start = ((), (), s32[]{:S(2)}) async-start(), calls=%async_computation.1 | async-start | bytes 6291456 | tf_op jit(solution)/shard_map/psum | solution.py:16
  8.7 11.4 %collective-permute-start = (bf16[16,6,512]{2,1,0:T(8,128)(2,1)S(1)}, bf16[16,6,512]{2,1,0:T(8,128)(2,1)S(1)}, u32[]{:S(2)}, u32[]{:S(2)}) collective-permute-start(bf16[16,6,512]{2,1,0:T(8,128)(2,1)S(1)} %get-tuple-element.230), channel_id=1, source_target_pairs={{0,1},{1,2},{2,3},{3,4},{4,5},{5,6},{6,7},{7,8},{8,9},{9,10},{10,1... | collective-permute-start | bytes 294920 | tf_op jit(solution)/shard_map/ppermute | solution.py:27
  13.2 7.1 collective-permute-start.1
  20.5 6.2 collective-permute-start.2
  24.1 7.9 collective-permute-start.3
  37.4 19.4 %copy-start.31 = (bf16[448,256]{1,0:T(8,128)(2,1)S(1)}, bf16[448,256]{1,0:T(8,128)(2,1)}, u32[]{:S(2)}) copy-start(bf16[448,256]{1,0:T(8,128)(2,1)} %get-tuple-element.212) | copy-start | bytes 688132
  37.4 20.1 %copy-start.30 = (bf16[448,256]{1,0:T(8,128)(2,1)S(1)}, bf16[448,256]{1,0:T(8,128)(2,1)}, u32[]{:S(2)}) copy-start(bf16[448,256]{1,0:T(8,128)(2,1)} %get-tuple-element.213) | copy-start | bytes 688132
  38.1 19.4 %copy-start.29 = (bf16[448,256]{1,0:T(8,128)(2,1)S(1)}, bf16[448,256]{1,0:T(8,128)(2,1)}, u32[]{:S(2)}) copy-start(bf16[448,256]{1,0:T(8,128)(2,1)} %get-tuple-element.214) | copy-start | bytes 688132
  63.7 13.1 %copy-start.21 = (bf16[16,1,28,256]{3,2,0,1:T(8,128)(2,1)S(1)}, bf16[16,1,28,256]{3,2,0,1:T(8,128)(2,1)}, u32[]{:S(2)}) copy-start(bf16[16,1,28,256]{3,2,0,1:T(8,128)(2,1)} %stack.108) | copy-start | bytes 688132
  63.7 13.9 %copy-start.19 = (bf16[16,1,28,256]{3,2,0,1:T(8,128)(2,1)S(1)}, bf16[16,1,28,256]{3,2,0,1:T(8,128)(2,1)}, u32[]{:S(2)}) copy-start(bf16[16,1,28,256]{3,2,0,1:T(8,128)(2,1)} %stack.109) | copy-start | bytes 688132
  63.7 14.6 %copy-start.17 = (bf16[16,1,28,256]{3,2,0,1:T(8,128)(2,1)S(1)}, bf16[16,1,28,256]{3,2,0,1:T(8,128)(2,1)}, u32[]{:S(2)}) copy-start(bf16[16,1,28,256]{3,2,0,1:T(8,128)(2,1)} %stack.110) | copy-start | bytes 688132
  352.5 21.3 %copy-start.7 = (bf16[256,1024]{1,0:T(8,128)(2,1)S(1)}, bf16[256,1024]{1,0:T(8,128)(2,1)}, u32[]{:S(2)}) copy-start(bf16[256,1024]{1,0:T(8,128)(2,1)} %copy-done.6) | copy-start | bytes 1572868
  352.5 9.9 %collective-permute-start.4 = (bf16[28,6,512]{2,0,1:T(8,128)(2,1)S(1)}, bf16[28,6,512]{2,0,1:T(8,128)(2,1)S(1)}, u32[]{:S(2)}, u32[]{:S(2)}) collective-permute-start(bf16[28,6,512]{2,0,1:T(8,128)(2,1)S(1)} %get-tuple-element.198), channel_id=1, source_target_pairs={{0,1},{1,2},{2,3},{3,4},{4,5},{5,6},{6,7},{7,8},{8,9},{9,10},{10,1... | collective-permute-start | bytes 516104 | tf_op jit(solution)/shard_map/ppermute | solution.py:27
  355.7 19.4 %copy-start.33 = (bf16[16,16,8,32]{3,1,2,0:T(8,128)(2,1)S(1)}, bf16[16,16,8,32]{3,1,2,0:T(8,128)(2,1)}, u32[]{:S(2)}) copy-start(bf16[16,16,8,32]{3,1,2,0:T(8,128)(2,1)} %fusion.20) | copy-start | bytes 393220
  355.7 7.1 collective-permute-start.5
  362.4 13.1 %copy-start.10 = (bf16[256,256]{1,0:T(8,128)(2,1)S(1)}, bf16[256,256]{1,0:T(8,128)(2,1)}, u32[]{:S(2)}) copy-start(bf16[256,256]{1,0:T(8,128)(2,1)} %copy-done.9) | copy-start | bytes 393220
  362.4 13.1 %copy-start.12 = (bf16[256,256]{1,0:T(8,128)(2,1)S(1)}, bf16[256,256]{1,0:T(8,128)(2,1)}, u32[]{:S(2)}) copy-start(bf16[256,256]{1,0:T(8,128)(2,1)} %copy-done.11) | copy-start | bytes 393220
  363.7 22.4 %collective-permute-start.6 = (bf16[6,40,512]{2,0,1:T(8,128)(2,1)}, bf16[6,40,512]{2,0,1:T(8,128)(2,1)S(1)}, u32[]{:S(2)}, u32[]{:S(2)}) collective-permute-start(bf16[6,40,512]{2,0,1:T(8,128)(2,1)} %get-tuple-element.196), channel_id=1, source_target_pairs={{0,32},{32,64},{64,96},{96,128},{128,160},{160,192},{192,224},{224... | collective-permute-start | bytes 737288 | tf_op jit(solution)/shard_map/ppermute | solution.py:27
  372.2 13.9 %collective-permute-start.7 = (bf16[6,40,512]{2,0,1:T(8,128)(2,1)}, bf16[6,40,512]{2,0,1:T(8,128)(2,1)S(1)}, u32[]{:S(2)}, u32[]{:S(2)}) collective-permute-start(bf16[6,40,512]{2,0,1:T(8,128)(2,1)} %get-tuple-element.197), channel_id=1, source_target_pairs={{32,0},{64,32},{96,64},{128,96},{160,128},{192,160},{224,192},{256... | collective-permute-start | bytes 737288 | tf_op jit(solution)/shard_map/ppermute | solution.py:28
  389.0 288.0 %copy-start.16 = (f32[256,256]{1,0:T(8,128)S(1)}, f32[256,256]{1,0:T(8,128)}, u32[]{:S(2)}) copy-start(f32[256,256]{1,0:T(8,128)} %copy-done.15) | copy-start | bytes 786436
  389.0 288.0 %copy-start.35 = (bf16[256,768]{1,0:T(8,128)(2,1)S(1)}, bf16[256,768]{1,0:T(8,128)(2,1)}, u32[]{:S(2)}) copy-start(bf16[256,768]{1,0:T(8,128)(2,1)} %param.35) | copy-start | bytes 1179652
  389.0 436.3 %all-reduce.10.cloned.1.call-start = ((), (), s32[]{:S(2)}) async-start(), calls=%async_computation | async-start | bytes 6291456 | tf_op jit(solution)/shard_map/psum | solution.py:16
  676.5 155.7 %copy-start.1 = (bf16[256,1024]{1,0:T(8,128)(2,1)S(1)}, bf16[256,1024]{1,0:T(8,128)(2,1)}, u32[]{:S(2)}) copy-start(bf16[256,1024]{1,0:T(8,128)(2,1)} %param.38) | copy-start | bytes 1572868
  (29 other events, 124.7 us)
Sparse Core Ops, SparseCore 0:
  389.2 187.0 all-reduce.11
  579.5 245.7 all-reduce.9
